TPU v7x, 32 devices: a whole 2x2x4 slice. The times are simulated.
32 devices in a mesh: pipe: 2 (over y), ctx: 16 (over z, x, core).
Axes of the slice: x: 2, y: 2, z: 4, core: 2. Of those that a mesh axis runs over, the one named last changes fastest.
Arguments:
- saved_qkv: bfloat16 [2, 3, 2048, 2048], P('pipe', None, 'ctx'), may hold values from -6 to 6
- handed: bfloat16 [2, 2048, 2048], P('pipe', 'ctx'), may hold values from -6 to 6
- long_filter: bfloat16 [2, 128, 128], P('pipe'), may hold values from -0.5 to 0.5
- short_filter: bfloat16 [2, 3, 3, 2048], P('pipe'), may hold values from -3.5 to 3.5
- doc_lengths: int32 [16], replicated, may hold values from 1 to 512, 2048 in all
Outputs:
- grad_pre: bfloat16 [2, 3, 2048, 2048], P('pipe', None, 'ctx')
- filter_grad: float32 [2, 128, 128], P('pipe')
Inputs may be any that keep to these rules, and one draw needn't show every extreme that they name: `doc_lengths`: documents lie end to end and sum to 2048 tokens; the longest has exactly 512 tokens.
All inputs are finite; a program needn't handle non-finite values.
Results may differ from a plain program's by a relative error of at most 0.0058.
Values may be sent and summed in bfloat16 or wider, within the bound.
A program may use at most 64 MiB of HBM per device.

v0:
```python
import math
import jax
import jax.numpy as jnp
from jax import lax
from jax.sharding import PartitionSpec as P


def from_behind(shard, axis, by):
    count = lax.axis_size(axis)
    return lax.ppermute(shard, axis, [(i, (i + by) % count) for i in range(count)])


def shifted_2(block, axis, distance):
    devices = range(lax.axis_size(axis))
    route = [(i - distance, i) for i in devices if i - distance in devices]
    return lax.ppermute(block, axis, route)


def back_conv(grad_rows, grad_pos, filt, out_len, members, unroll):
    tap_count = filt.shape[0]
    channels = grad_rows.shape[1]

    def step(total, base):
        for offset in range(unroll):
            lag = base * unroll + offset
            ahead = lax.dynamic_slice_in_dim(grad_rows, lag, out_len, 0).astype(jnp.float32)
            ahead_pos = lax.dynamic_slice_in_dim(grad_pos, lag, out_len, 0)
            weights = jnp.repeat(filt[lag].astype(jnp.float32), members)
            total = total + jnp.where((lag <= ahead_pos)[:, None], ahead * weights[None, :], 0.0)
        return (total, None)

    bases = jnp.arange(tap_count // unroll, dtype=jnp.int32)
    result, _ = lax.scan(step, jnp.zeros((out_len, channels), jnp.float32), bases)
    return result


def body(saved_qkv, handed, long_filter, short_filter, doc_lengths):
    query_rows = saved_qkv[0, 0]
    key_rows = saved_qkv[0, 1]
    value_rows = saved_qkv[0, 2]
    filt = long_filter[0]
    tap_count, groups = filt.shape
    row_count, channels = query_rows.shape
    members = channels // groups
    short_taps = short_filter.shape[2]
    unroll = math.gcd(tap_count, 16)
    devices = lax.axis_size("ctx")
    device_index = lax.axis_index("ctx")
    starts = jnp.cumsum(doc_lengths) - doc_lengths
    global_rows = device_index * row_count + jnp.arange(row_count + tap_count, dtype=jnp.int32)
    latest = jnp.max(jnp.where(starts[None, :] <= global_rows[:, None], starts[None, :], 0), axis=1)
    position = global_rows - latest
    own_pos = position[:row_count]
    incoming = from_behind(handed[0], "pipe", -1)
    product = (key_rows.astype(jnp.float32) * value_rows.astype(jnp.float32)).astype(jnp.bfloat16)
    tail_rows = shifted_2(product, "ctx", 1)
    extended = jnp.concatenate([tail_rows, product], axis=0)
    conv_grad = (incoming.astype(jnp.float32) * query_rows.astype(jnp.float32)).astype(jnp.bfloat16)
    grad_wide = conv_grad.astype(jnp.float32)

    def forward_step(total, base):
        columns = []
        for offset in range(unroll):
            lag = base * unroll + offset
            shifted = lax.dynamic_slice_in_dim(extended, tap_count - lag, row_count, 0).astype(
                jnp.float32
            )
            weights = jnp.repeat(filt[lag].astype(jnp.float32), members)
            usable = (lag <= own_pos)[:, None]
            total = total + jnp.where(usable, shifted * weights[None, :], 0.0)
            pair = jnp.sum(
                (grad_wide * shifted).reshape(row_count, groups, members), axis=2
            ).astype(jnp.bfloat16)
            pair = lax.optimization_barrier(pair).astype(jnp.float32)
            columns.append(jnp.sum(jnp.where(usable, pair, 0.0), axis=0))
        return (total, jnp.stack(columns))

    bases = jnp.arange(tap_count // unroll, dtype=jnp.int32)
    conv_out, filter_cols = lax.scan(
        forward_step, jnp.zeros((row_count, channels), jnp.float32), bases
    )
    filter_sum = filter_cols.reshape(tap_count, groups)
    head_rows = shifted_2(conv_grad, "ctx", -1)
    joined = jnp.concatenate([conv_grad, head_rows], axis=0)
    own_grad = back_conv(joined, position, filt, row_count, members, unroll)
    query_grad = (incoming.astype(jnp.float32) * conv_out).astype(jnp.bfloat16)
    key_grad = (own_grad * value_rows.astype(jnp.float32)).astype(jnp.bfloat16)
    value_grad = (own_grad * key_rows.astype(jnp.float32)).astype(jnp.bfloat16)
    stacked = jnp.stack([query_grad, key_grad, value_grad])
    rim_rows = shifted_2(stacked[:, : short_taps - 1], "ctx", -1)
    stacked_ext = jnp.concatenate([stacked, rim_rows], axis=1)
    weights_all = short_filter[0]
    total = jnp.zeros((3, row_count, channels), jnp.float32)
    for shift_by in range(short_taps):
        usable = (shift_by <= position[shift_by : shift_by + row_count])[None, :, None]
        weights = weights_all[:, shift_by].astype(jnp.float32)[:, None, :]
        total = total + jnp.where(
            usable,
            weights * stacked_ext[:, shift_by : shift_by + row_count].astype(jnp.float32),
            0.0,
        )
    grad_pre = total.astype(jnp.bfloat16)[None]
    summed = lax.psum(filter_sum, "ctx")
    filter_grad = (summed / math.sqrt(row_count * devices * members))[None]
    return (grad_pre, filter_grad)


def solution(mesh):
    return jax.shard_map(
        body,
        mesh=mesh,
        in_specs=(
            P("pipe", None, "ctx", None),
            P("pipe", "ctx", None),
            P("pipe", None, None),
            P("pipe", None, None, None),
            P(),
        ),
        out_specs=(P("pipe", None, "ctx", None), P("pipe", None, None)),
        check_vma=False,
    )
```

profile of v0, /device:TPU:8, one launch (start us, length us, event | category | flops | bytes accessed | tf_op | source)
XLA Modules:
  0.0 410.6 jit_solution(385893030262521515)
XLA Ops:
  7.2 1.6 collective-permute-start
  8.8 12.4 %collective-permute-done = bf16[128,2048]{1,0:T(8,128)(2,1)S(1)} collective-permute-done((bf16[128,2048]{1,0:T(8,128)(2,1)}, bf16[128,2048]{1,0:T(8,128)(2,1)S(1)}, u32[]{:S(2)}, u32[]{:S(2)}) %collective-permute-start) | collective-permute-done | bytes 524320 | tf_op jit(solution)/shard_map/ppermute | solution.py:10
  21.2 1.4 fusion.112
  22.6 1.9 collective-permute-start.2
  24.5 0.7 copy.16
  26.2 5.0 %collective-permute-done.2 = bf16[128,2048]{1,0:T(8,128)(2,1)S(1)} collective-permute-done((bf16[128,2048]{1,0:T(8,128)(2,1)S(1)}, bf16[128,2048]{1,0:T(8,128)(2,1)S(1)}, u32[]{:S(2)}, u32[]{:S(2)}) %collective-permute-start.2) | collective-permute-done | bytes 524320 | tf_op jit(solution)/shard_map/ppermute | solution.py:16
  31.3 81.4 %while.30 = (s32[]{:T(128)}, f32[128,2048]{1,0:T(8,128)S(1)}, s32[8]{0:T(128)S(1)}, s32[256]{0:T(256)S(1)}, bf16[256,2048]{1,0:T(8,128)(2,1)S(1)}, /*index=5*/bf...) while((s32[]{:T(128)}, f32[128,2048]{1,0:T(8,128)S(1)}, ...), condition=%wide.region_37.38_spmd.clone, body=%wide.region_36.37_spmd.clone.sunk | while | flops 17043556 | bytes 11044691 | solution.py:33
  31.3 0.7 dynamic_slice.941
  35.9 5.6 %fusion.128 = f32[128,2048]{1,0:T(8,128)S(1)} fusion(f32[128,2048]{1,0:T(8,128)S(1)} %get-tuple-element.835, f32[2048]{0:T(1024)S(1)} %mul.1435, bf16[256,2048]{1,0:T(8,128)(2,1)S(1)} %get-tuple-element.893, s32[]{:T(128)S(6)} %select_n.1196, f32[2048]{0:T(1024)S(1)} %mul.1436, s32[]{:T(128)S(6)} %select_n.1197, f32[2048]{0:T(1024)S(1)} %mul.1437, ...), kind=kLoop, calls=%fused_computation.176.clone.1 | loop fusion | flops 17039360 | bytes 10618945 | tf_op jit(solution)/shard_map/while/body/eval_jaxpr/add | solution.py:29
  41.5 0.7 dynamic_slice.941
  46.1 5.6 %fusion.128 = f32[128,2048]{1,0:T(8,128)S(1)} fusion(f32[128,2048]{1,0:T(8,128)S(1)} %get-tuple-element.835, f32[2048]{0:T(1024)S(1)} %mul.1435, bf16[256,2048]{1,0:T(8,128)(2,1)S(1)} %get-tuple-element.893, s32[]{:T(128)S(6)} %select_n.1196, f32[2048]{0:T(1024)S(1)} %mul.1436, s32[]{:T(128)S(6)} %select_n.1197, f32[2048]{0:T(1024)S(1)} %mul.1437, ...), kind=kLoop, calls=%fused_computation.176.clone.1 | loop fusion | flops 17039360 | bytes 10618945 | tf_op jit(solution)/shard_map/while/body/eval_jaxpr/add | solution.py:29
  51.7 0.7 dynamic_slice.941
  56.2 5.6 %fusion.128 = f32[128,2048]{1,0:T(8,128)S(1)} fusion(f32[128,2048]{1,0:T(8,128)S(1)} %get-tuple-element.835, f32[2048]{0:T(1024)S(1)} %mul.1435, bf16[256,2048]{1,0:T(8,128)(2,1)S(1)} %get-tuple-element.893, s32[]{:T(128)S(6)} %select_n.1196, f32[2048]{0:T(1024)S(1)} %mul.1436, s32[]{:T(128)S(6)} %select_n.1197, f32[2048]{0:T(1024)S(1)} %mul.1437, ...), kind=kLoop, calls=%fused_computation.176.clone.1 | loop fusion | flops 17039360 | bytes 10618945 | tf_op jit(solution)/shard_map/while/body/eval_jaxpr/add | solution.py:29
  61.9 0.7 dynamic_slice.941
  66.4 5.6 %fusion.128 = f32[128,2048]{1,0:T(8,128)S(1)} fusion(f32[128,2048]{1,0:T(8,128)S(1)} %get-tuple-element.835, f32[2048]{0:T(1024)S(1)} %mul.1435, bf16[256,2048]{1,0:T(8,128)(2,1)S(1)} %get-tuple-element.893, s32[]{:T(128)S(6)} %select_n.1196, f32[2048]{0:T(1024)S(1)} %mul.1436, s32[]{:T(128)S(6)} %select_n.1197, f32[2048]{0:T(1024)S(1)} %mul.1437, ...), kind=kLoop, calls=%fused_computation.176.clone.1 | loop fusion | flops 17039360 | bytes 10618945 | tf_op jit(solution)/shard_map/while/body/eval_jaxpr/add | solution.py:29
  72.0 0.7 dynamic_slice.941
  76.6 5.6 %fusion.128 = f32[128,2048]{1,0:T(8,128)S(1)} fusion(f32[128,2048]{1,0:T(8,128)S(1)} %get-tuple-element.835, f32[2048]{0:T(1024)S(1)} %mul.1435, bf16[256,2048]{1,0:T(8,128)(2,1)S(1)} %get-tuple-element.893, s32[]{:T(128)S(6)} %select_n.1196, f32[2048]{0:T(1024)S(1)} %mul.1436, s32[]{:T(128)S(6)} %select_n.1197, f32[2048]{0:T(1024)S(1)} %mul.1437, ...), kind=kLoop, calls=%fused_computation.176.clone.1 | loop fusion | flops 17039360 | bytes 10618945 | tf_op jit(solution)/shard_map/while/body/eval_jaxpr/add | solution.py:29
  86.7 5.6 %fusion.128 = f32[128,2048]{1,0:T(8,128)S(1)} fusion(f32[128,2048]{1,0:T(8,128)S(1)} %get-tuple-element.835, f32[2048]{0:T(1024)S(1)} %mul.1435, bf16[256,2048]{1,0:T(8,128)(2,1)S(1)} %get-tuple-element.893, s32[]{:T(128)S(6)} %select_n.1196, f32[2048]{0:T(1024)S(1)} %mul.1436, s32[]{:T(128)S(6)} %select_n.1197, f32[2048]{0:T(1024)S(1)} %mul.1437, ...), kind=kLoop, calls=%fused_computation.176.clone.1 | loop fusion | flops 17039360 | bytes 10618945 | tf_op jit(solution)/shard_map/while/body/eval_jaxpr/add | solution.py:29
  96.9 5.6 %fusion.128 = f32[128,2048]{1,0:T(8,128)S(1)} fusion(f32[128,2048]{1,0:T(8,128)S(1)} %get-tuple-element.835, f32[2048]{0:T(1024)S(1)} %mul.1435, bf16[256,2048]{1,0:T(8,128)(2,1)S(1)} %get-tuple-element.893, s32[]{:T(128)S(6)} %select_n.1196, f32[2048]{0:T(1024)S(1)} %mul.1436, s32[]{:T(128)S(6)} %select_n.1197, f32[2048]{0:T(1024)S(1)} %mul.1437, ...), kind=kLoop, calls=%fused_computation.176.clone.1 | loop fusion | flops 17039360 | bytes 10618945 | tf_op jit(solution)/shard_map/while/body/eval_jaxpr/add | solution.py:29
  107.1 5.6 %fusion.128 = f32[128,2048]{1,0:T(8,128)S(1)} fusion(f32[128,2048]{1,0:T(8,128)S(1)} %get-tuple-element.835, f32[2048]{0:T(1024)S(1)} %mul.1435, bf16[256,2048]{1,0:T(8,128)(2,1)S(1)} %get-tuple-element.893, s32[]{:T(128)S(6)} %select_n.1196, f32[2048]{0:T(1024)S(1)} %mul.1436, s32[]{:T(128)S(6)} %select_n.1197, f32[2048]{0:T(1024)S(1)} %mul.1437, ...), kind=kLoop, calls=%fused_computation.176.clone.1 | loop fusion | flops 17039360 | bytes 10618945 | tf_op jit(solution)/shard_map/while/body/eval_jaxpr/add | solution.py:29
  112.7 2.6 fusion.118
  115.3 3.8 collective-permute-start.1
  119.5 7.5 %collective-permute-done.1 = bf16[128,2048]{1,0:T(8,128)(2,1)} collective-permute-done((bf16[128,2048]{1,0:T(8,128)(2,1)S(1)}, bf16[128,2048]{1,0:T(8,128)(2,1)}, u32[]{:S(2)}, u32[]{:S(2)}) %collective-permute-start.1) | collective-permute-done | bytes 524320 | tf_op jit(solution)/shard_map/ppermute | solution.py:16
  127.0 2.2 pad_maximum_fusion.2
  129.1 1.5 copy.17
  130.6 178.6 %while.29 = (s32[]{:T(128)}, f32[128,2048]{0,1:T(8,128)S(1)}, f32[8,16,128]{2,1,0:T(8,128)}, s32[8]{0:T(128)S(1)}, s32[128]{0:T(128)S(1)}, /*index=5*/bf16[256,2...) while((s32[]{:T(128)}, f32[128,2048]{0,1:T(8,128)S(1)}, ...), condition=%wide.region_35.36_spmd.clone, body=%wide.region_2.35_spmd.clone.sunk | while | flops 30148740 | bytes 21566524 | solution.py:79
  132.0 6.9 %bitcast_reduce_fusion.17 = (bf16[128,128]{0,1:T(8,128)(2,1)S(1)}, bf16[128,128]{0,1:T(8,128)(2,1)S(1)}, bf16[128,128]{0,1:T(8,128)(2,1)S(1)}, bf16[128,128]{0,1...) fusion(f32[128,2048]{0,1:T(8,128)S(1)} %get-tuple-element.1035,, ...), kind=kLoop, calls=%fused_computation.64.clone.1 | loop fusion | flops 12320768 | bytes 9961536 | tf_op jit(solution)/shard_map/while/body/eval_jaxpr/reduce_sum | solution.py:71
  143.3 9.6 %fusion.126 = f32[128,2048]{0,1:T(8,128)S(1)} fusion(f32[128,2048]{0,1:T(8,128)S(1)} %get-tuple-element.987, f32[2048]{0:T(1024)S(1)} %mul.1386, f32[2048]{0:T(1024)S(1)} %mul.1387, f32[2048]{0:T(1024)S(1)} %mul.1388, f32[2048]{0:T(1024)S(1)} %mul.1389, f32[2048]{0:T(1024)S(1)} %mul.1390, f32[2048]{0:T(1024)S(1)} %mul.1391, f32[2048]{0:T(1024)S(1)} %mul.1392, ...), kind=kLoop, calls=%fused_computation.48.clone.1 | loop fusion | flops 17039360 | bytes 10618945 | tf_op jit(solution)/shard_map/while/body/eval_jaxpr/add | solution.py:70
  154.3 6.9 %bitcast_reduce_fusion.17 = (bf16[128,128]{0,1:T(8,128)(2,1)S(1)}, bf16[128,128]{0,1:T(8,128)(2,1)S(1)}, bf16[128,128]{0,1:T(8,128)(2,1)S(1)}, bf16[128,128]{0,1...) fusion(f32[128,2048]{0,1:T(8,128)S(1)} %get-tuple-element.1035,, ...), kind=kLoop, calls=%fused_computation.64.clone.1 | loop fusion | flops 12320768 | bytes 9961536 | tf_op jit(solution)/shard_map/while/body/eval_jaxpr/reduce_sum | solution.py:71
  165.7 9.6 %fusion.126 = f32[128,2048]{0,1:T(8,128)S(1)} fusion(f32[128,2048]{0,1:T(8,128)S(1)} %get-tuple-element.987, f32[2048]{0:T(1024)S(1)} %mul.1386, f32[2048]{0:T(1024)S(1)} %mul.1387, f32[2048]{0:T(1024)S(1)} %mul.1388, f32[2048]{0:T(1024)S(1)} %mul.1389, f32[2048]{0:T(1024)S(1)} %mul.1390, f32[2048]{0:T(1024)S(1)} %mul.1391, f32[2048]{0:T(1024)S(1)} %mul.1392, ...), kind=kLoop, calls=%fused_computation.48.clone.1 | loop fusion | flops 17039360 | bytes 10618945 | tf_op jit(solution)/shard_map/while/body/eval_jaxpr/add | solution.py:70
  176.7 6.9 %bitcast_reduce_fusion.17 = (bf16[128,128]{0,1:T(8,128)(2,1)S(1)}, bf16[128,128]{0,1:T(8,128)(2,1)S(1)}, bf16[128,128]{0,1:T(8,128)(2,1)S(1)}, bf16[128,128]{0,1...) fusion(f32[128,2048]{0,1:T(8,128)S(1)} %get-tuple-element.1035,, ...), kind=kLoop, calls=%fused_computation.64.clone.1 | loop fusion | flops 12320768 | bytes 9961536 | tf_op jit(solution)/shard_map/while/body/eval_jaxpr/reduce_sum | solution.py:71
  188.0 9.6 %fusion.126 = f32[128,2048]{0,1:T(8,128)S(1)} fusion(f32[128,2048]{0,1:T(8,128)S(1)} %get-tuple-element.987, f32[2048]{0:T(1024)S(1)} %mul.1386, f32[2048]{0:T(1024)S(1)} %mul.1387, f32[2048]{0:T(1024)S(1)} %mul.1388, f32[2048]{0:T(1024)S(1)} %mul.1389, f32[2048]{0:T(1024)S(1)} %mul.1390, f32[2048]{0:T(1024)S(1)} %mul.1391, f32[2048]{0:T(1024)S(1)} %mul.1392, ...), kind=kLoop, calls=%fused_computation.48.clone.1 | loop fusion | flops 17039360 | bytes 10618945 | tf_op jit(solution)/shard_map/while/body/eval_jaxpr/add | solution.py:70
  199.0 6.9 %bitcast_reduce_fusion.17 = (bf16[128,128]{0,1:T(8,128)(2,1)S(1)}, bf16[128,128]{0,1:T(8,128)(2,1)S(1)}, bf16[128,128]{0,1:T(8,128)(2,1)S(1)}, bf16[128,128]{0,1...) fusion(f32[128,2048]{0,1:T(8,128)S(1)} %get-tuple-element.1035,, ...), kind=kLoop, calls=%fused_computation.64.clone.1 | loop fusion | flops 12320768 | bytes 9961536 | tf_op jit(solution)/shard_map/while/body/eval_jaxpr/reduce_sum | solution.py:71
  210.3 9.6 %fusion.126 = f32[128,2048]{0,1:T(8,128)S(1)} fusion(f32[128,2048]{0,1:T(8,128)S(1)} %get-tuple-element.987, f32[2048]{0:T(1024)S(1)} %mul.1386, f32[2048]{0:T(1024)S(1)} %mul.1387, f32[2048]{0:T(1024)S(1)} %mul.1388, f32[2048]{0:T(1024)S(1)} %mul.1389, f32[2048]{0:T(1024)S(1)} %mul.1390, f32[2048]{0:T(1024)S(1)} %mul.1391, f32[2048]{0:T(1024)S(1)} %mul.1392, ...), kind=kLoop, calls=%fused_computation.48.clone.1 | loop fusion | flops 17039360 | bytes 10618945 | tf_op jit(solution)/shard_map/while/body/eval_jaxpr/add | solution.py:70
  221.3 6.9 %bitcast_reduce_fusion.17 = (bf16[128,128]{0,1:T(8,128)(2,1)S(1)}, bf16[128,128]{0,1:T(8,128)(2,1)S(1)}, bf16[128,128]{0,1:T(8,128)(2,1)S(1)}, bf16[128,128]{0,1...) fusion(f32[128,2048]{0,1:T(8,128)S(1)} %get-tuple-element.1035,, ...), kind=kLoop, calls=%fused_computation.64.clone.1 | loop fusion | flops 12320768 | bytes 9961536 | tf_op jit(solution)/shard_map/while/body/eval_jaxpr/reduce_sum | solution.py:71
  232.7 9.6 %fusion.126 = f32[128,2048]{0,1:T(8,128)S(1)} fusion(f32[128,2048]{0,1:T(8,128)S(1)} %get-tuple-element.987, f32[2048]{0:T(1024)S(1)} %mul.1386, f32[2048]{0:T(1024)S(1)} %mul.1387, f32[2048]{0:T(1024)S(1)} %mul.1388, f32[2048]{0:T(1024)S(1)} %mul.1389, f32[2048]{0:T(1024)S(1)} %mul.1390, f32[2048]{0:T(1024)S(1)} %mul.1391, f32[2048]{0:T(1024)S(1)} %mul.1392, ...), kind=kLoop, calls=%fused_computation.48.clone.1 | loop fusion | flops 17039360 | bytes 10618945 | tf_op jit(solution)/shard_map/while/body/eval_jaxpr/add | solution.py:70
  243.6 6.9 %bitcast_reduce_fusion.17 = (bf16[128,128]{0,1:T(8,128)(2,1)S(1)}, bf16[128,128]{0,1:T(8,128)(2,1)S(1)}, bf16[128,128]{0,1:T(8,128)(2,1)S(1)}, bf16[128,128]{0,1...) fusion(f32[128,2048]{0,1:T(8,128)S(1)} %get-tuple-element.1035,, ...), kind=kLoop, calls=%fused_computation.64.clone.1 | loop fusion | flops 12320768 | bytes 9961536 | tf_op jit(solution)/shard_map/while/body/eval_jaxpr/reduce_sum | solution.py:71
  255.0 9.6 %fusion.126 = f32[128,2048]{0,1:T(8,128)S(1)} fusion(f32[128,2048]{0,1:T(8,128)S(1)} %get-tuple-element.987, f32[2048]{0:T(1024)S(1)} %mul.1386, f32[2048]{0:T(1024)S(1)} %mul.1387, f32[2048]{0:T(1024)S(1)} %mul.1388, f32[2048]{0:T(1024)S(1)} %mul.1389, f32[2048]{0:T(1024)S(1)} %mul.1390, f32[2048]{0:T(1024)S(1)} %mul.1391, f32[2048]{0:T(1024)S(1)} %mul.1392, ...), kind=kLoop, calls=%fused_computation.48.clone.1 | loop fusion | flops 17039360 | bytes 10618945 | tf_op jit(solution)/shard_map/while/body/eval_jaxpr/add | solution.py:70
  266.0 6.9 %bitcast_reduce_fusion.17 = (bf16[128,128]{0,1:T(8,128)(2,1)S(1)}, bf16[128,128]{0,1:T(8,128)(2,1)S(1)}, bf16[128,128]{0,1:T(8,128)(2,1)S(1)}, bf16[128,128]{0,1...) fusion(f32[128,2048]{0,1:T(8,128)S(1)} %get-tuple-element.1035,, ...), kind=kLoop, calls=%fused_computation.64.clone.1 | loop fusion | flops 12320768 | bytes 9961536 | tf_op jit(solution)/shard_map/while/body/eval_jaxpr/reduce_sum | solution.py:71
  277.3 9.6 %fusion.126 = f32[128,2048]{0,1:T(8,128)S(1)} fusion(f32[128,2048]{0,1:T(8,128)S(1)} %get-tuple-element.987, f32[2048]{0:T(1024)S(1)} %mul.1386, f32[2048]{0:T(1024)S(1)} %mul.1387, f32[2048]{0:T(1024)S(1)} %mul.1388, f32[2048]{0:T(1024)S(1)} %mul.1389, f32[2048]{0:T(1024)S(1)} %mul.1390, f32[2048]{0:T(1024)S(1)} %mul.1391, f32[2048]{0:T(1024)S(1)} %mul.1392, ...), kind=kLoop, calls=%fused_computation.48.clone.1 | loop fusion | flops 17039360 | bytes 10618945 | tf_op jit(solution)/shard_map/while/body/eval_jaxpr/add | solution.py:70
  288.3 6.9 %bitcast_reduce_fusion.17 = (bf16[128,128]{0,1:T(8,128)(2,1)S(1)}, bf16[128,128]{0,1:T(8,128)(2,1)S(1)}, bf16[128,128]{0,1:T(8,128)(2,1)S(1)}, bf16[128,128]{0,1...) fusion(f32[128,2048]{0,1:T(8,128)S(1)} %get-tuple-element.1035,, ...), kind=kLoop, calls=%fused_computation.64.clone.1 | loop fusion | flops 12320768 | bytes 9961536 | tf_op jit(solution)/shard_map/while/body/eval_jaxpr/reduce_sum | solution.py:71
  299.6 9.6 %fusion.126 = f32[128,2048]{0,1:T(8,128)S(1)} fusion(f32[128,2048]{0,1:T(8,128)S(1)} %get-tuple-element.987, f32[2048]{0:T(1024)S(1)} %mul.1386, f32[2048]{0:T(1024)S(1)} %mul.1387, f32[2048]{0:T(1024)S(1)} %mul.1388, f32[2048]{0:T(1024)S(1)} %mul.1389, f32[2048]{0:T(1024)S(1)} %mul.1390, f32[2048]{0:T(1024)S(1)} %mul.1391, f32[2048]{0:T(1024)S(1)} %mul.1392, ...), kind=kLoop, calls=%fused_computation.48.clone.1 | loop fusion | flops 17039360 | bytes 10618945 | tf_op jit(solution)/shard_map/while/body/eval_jaxpr/add | solution.py:70
  309.6 1.2 fusion.119
  311.0 1.9 collective-permute-start.3
  313.0 1.4 collective-permute-done.3
  314.6 2.6 fusion.111
  317.2 85.1 %all-reduce.2.cloned.1.call-done = f32[128,128]{1,0:T(8,128)} async-done(((f32[128,128]{1,0:T(8,128)}), f32[128,128]{1,0:T(8,128)}) %all-reduce.2.cloned.1.call-update) | async-done | bytes 65552 | tf_op jit(solution)/shard_map/psum | solution.py:103
  402.2 1.5 multiply_bitcast_fusion
  (681 shorter events, 67.4 us)
Async XLA Ops:
  7.2 395.1 %all-reduce.2.cloned.1.call-start = ((), (), s32[]{:S(2)}) async-start(), calls=%async_computation | async-start | bytes 131072 | tf_op jit(solution)/shard_map/psum | solution.py:103
  7.2 24.1 %copy-start.5 = (bf16[1,128,128]{2,1,0:T(8,128)(2,1)S(1)}, bf16[1,128,128]{2,1,0:T(8,128)(2,1)}, u32[]{:S(2)}) copy-start(bf16[1,128,128]{2,1,0:T(8,128)(2,1)} %param.11) | copy-start | bytes 98308
  7.2 13.9 %collective-permute-start = (bf16[128,2048]{1,0:T(8,128)(2,1)}, bf16[128,2048]{1,0:T(8,128)(2,1)S(1)}, u32[]{:S(2)}, u32[]{:S(2)}) collective-permute-start(bf16[128,2048]{1,0:T(8,128)(2,1)} %bitcast.309), channel_id=1, source_target_pairs={{0,16},{16,0},{1,17},{17,1},{2,18},{18,2},{3,19},{19,3},{4,20},{20... | collective-permute-start | bytes 1572872 | tf_op jit(solution)/shard_map/ppermute | solution.py:10
  21.2 3.4 copy-start.4
  22.6 8.7 %copy-start.2 = (bf16[128,2048]{1,0:T(8,128)(2,1)}, bf16[128,2048]{1,0:T(8,128)(2,1)S(1)}, u32[]{:S(2)}) copy-start(bf16[128,2048]{1,0:T(8,128)(2,1)S(1)} %fusion.112) | copy-start | bytes 1572868
  22.6 8.6 %collective-permute-start.2 = (bf16[128,2048]{1,0:T(8,128)(2,1)S(1)}, bf16[128,2048]{1,0:T(8,128)(2,1)S(1)}, u32[]{:S(2)}, u32[]{:S(2)}) collective-permute-start(bf16[128,2048]{1,0:T(8,128)(2,1)S(1)} %fusion.112), channel_id=1, source_target_pairs={{1,0},{2,1},{3,2},{4,3},{5,4},{6,5},{7,6},{8,7},{9,8},{10,9},{11,1... | collective-permute-start | bytes 1572872 | tf_op jit(solution)/shard_map/ppermute | solution.py:16
  112.7 6.4 %copy-start.6 = (bf16[1,3,3,2048]{3,2,1,0:T(4,128)(2,1)S(1)}, bf16[1,3,3,2048]{3,2,1,0:T(4,128)(2,1)}, u32[]{:S(2)}) copy-start(bf16[1,3,3,2048]{3,2,1,0:T(4,128)(2,1)} %param.12) | copy-start | bytes 110596
  112.7 6.6 %copy-start.3 = (bf16[128,2048]{1,0:T(8,128)(2,1)S(1)}, bf16[128,2048]{1,0:T(8,128)(2,1)}, u32[]{:S(2)}) copy-start(bf16[128,2048]{1,0:T(8,128)(2,1)} %copy-done.2) | copy-start | bytes 1572868
  115.3 11.7 %collective-permute-start.1 = (bf16[128,2048]{1,0:T(8,128)(2,1)S(1)}, bf16[128,2048]{1,0:T(8,128)(2,1)}, u32[]{:S(2)}, u32[]{:S(2)}) collective-permute-start(bf16[128,2048]{1,0:T(8,128)(2,1)S(1)} %get-tuple-element.492), channel_id=1, source_target_pairs={{0,1},{1,2},{2,3},{3,4},{4,5},{5,6},{6,7},{7,8},{8,9},{9,10},{10,1... | collective-permute-start | bytes 1572872 | tf_op jit(solution)/shard_map/ppermute | solution.py:16
  309.2 1.5 copy-start
  309.2 1.5 copy-start.1
  311.0 3.4 collective-permute-start.3
Sparse Core Ops, SparseCore 0:
  313.2 89.0 all-reduce.1
where the time goes:
time: 411 us
  other arithmetic  200 us (49%)
  waiting for transfers between devices  111 us (27%)
  local copies, waits for them, and re-layouts  61.2 us (15%)
  between operations  14.3 us (3%)
  loops' own time  14.2 us (3%)
  starting transfers between devices  9.31 us (2%)
    psum x1, waiting for transfers between devices, body(): summed = lax.psum(filter_sum, 'ctx')  85.1 us
    add x8, other arithmetic, forward_step(): total = total + jnp.where(usable, shifted * weights[None, :], 0.0)  76.8 us
    reduce_sum x8, other arithmetic, forward_step(): jnp.sum((grad_wide * shifted).reshape(row_count, groups, members), axis=2)  55.5 us
    add x8, other arithmetic, step(): total + jnp.where((lag <= ahead_pos)[:, None], ahead * weights[None, :],...  44.8 us
    ppermute x3, waiting for transfers between devices, shifted_2(): return lax.ppermute(block, axis, route)  13.8 us
    ppermute x1, waiting for transfers between devices, from_behind(): lax.ppermute(shard, axis, [(i, (i + by) % count) for i in range(count)])  12.4 us
    mul x128, local copies, waits for them, and re-layouts, step(): ahead * weights[None, :]  12.2 us
    mul x128, local copies, waits for them, and re-layouts, forward_step(): total = total + jnp.where(usable, shifted * weights[None, :], 0.0)  12.2 us
  transfers between devices with their start and end apart: 5, of which 5 were waited for; matrix products, arithmetic and copies ran while one was open for 1% of the time, Pallas kernels for 0%

commit v1 on v0

--- a/solution.py
+++ b/solution.py
@@ -100,7 +100,7 @@
             0.0,
         )
     grad_pre = total.astype(jnp.bfloat16)[None]
-    summed = lax.psum(filter_sum, "ctx")
+    summed = jnp.sum(lax.all_gather(filter_sum, "ctx"), axis=0)
     filter_grad = (summed / math.sqrt(row_count * devices * members))[None]
     return (grad_pre, filter_grad)
 

time: 411 us -> 358 us (0.87)
  waiting for transfers between devices: 111 us -> 55.6 us
    psum x1 -> x0, waiting for transfers between devices: 85.1 us -> none  [body(): summed = lax.psum(filter_sum, 'ctx')]
    all_gather x0 -> x1, waiting for transfers between devices: none -> 29.3 us  [body(): summed = jnp.sum(lax.all_gather(filter_sum, 'ctx'), axis=0)]
  transfers between devices with their start and end apart: 5 -> 5, of which waited for: 5 -> 5; matrix products, arithmetic and copies ran while one was open for 1% -> 2% of each run, Pallas kernels for 0% -> 0%
where the time goes in v1:
time: 358 us; the launch traced here: 355 us
  other arithmetic  200 us (56%)
  local copies, waits for them, and re-layouts  61.2 us (17%)
  waiting for transfers between devices  55.6 us (16%)
  between operations  14.3 us (4%)
  loops' own time  14.2 us (4%)
  starting transfers between devices  9.31 us (3%)
    add x8, other arithmetic, forward_step(): total = total + jnp.where(usable, shifted * weights[None, :], 0.0)  76.4 us
    reduce_sum x8, other arithmetic, forward_step(): jnp.sum((grad_wide * shifted).reshape(row_count, groups, members), axis=2)  55 us
    add x8, other arithmetic, step(): total + jnp.where((lag <= ahead_pos)[:, None], ahead * weights[None, :],...  44.8 us
    all_gather x1, waiting for transfers between devices, body(): summed = jnp.sum(lax.all_gather(filter_sum, 'ctx'), axis=0)  29.3 us
    ppermute x3, waiting for transfers between devices, shifted_2(): return lax.ppermute(block, axis, route)  13.9 us
    ppermute x1, waiting for transfers between devices, from_behind(): lax.ppermute(shard, axis, [(i, (i + by) % count) for i in range(count)])  12.4 us
    mul x128, local copies, waits for them, and re-layouts, forward_step(): total = total + jnp.where(usable, shifted * weights[None, :], 0.0)  12.2 us
    mul x128, local copies, waits for them, and re-layouts, step(): ahead * weights[None, :]  12.2 us
  transfers between devices with their start and end apart: 5, of which 5 were waited for; matrix products, arithmetic and copies ran while one was open for 2% of the time, Pallas kernels for 0%

profile of v1, /device:TPU:8, one launch (start us, length us, event | category | flops | bytes accessed | tf_op | source)
XLA Modules:
  0.0 354.5 jit_solution(16049538584396699361)
XLA Ops:
  7.2 1.6 collective-permute-start
  8.8 12.4 %collective-permute-done = bf16[128,2048]{1,0:T(8,128)(2,1)S(1)} collective-permute-done((bf16[128,2048]{1,0:T(8,128)(2,1)}, bf16[128,2048]{1,0:T(8,128)(2,1)S(1)}, u32[]{:S(2)}, u32[]{:S(2)}) %collective-permute-start) | collective-permute-done | bytes 524320 | tf_op jit(solution)/shard_map/ppermute | solution.py:10
  21.2 1.4 fusion.112
  22.6 1.9 collective-permute-start.2
  24.5 0.7 copy.16
  26.2 5.0 %collective-permute-done.2 = bf16[128,2048]{1,0:T(8,128)(2,1)S(1)} collective-permute-done((bf16[128,2048]{1,0:T(8,128)(2,1)S(1)}, bf16[128,2048]{1,0:T(8,128)(2,1)S(1)}, u32[]{:S(2)}, u32[]{:S(2)}) %collective-permute-start.2) | collective-permute-done | bytes 524320 | tf_op jit(solution)/shard_map/ppermute | solution.py:16
  31.3 81.3 %while.30 = (s32[]{:T(128)}, f32[128,2048]{1,0:T(8,128)S(1)}, s32[8]{0:T(128)S(1)}, s32[256]{0:T(256)S(1)}, bf16[256,2048]{1,0:T(8,128)(2,1)S(1)}, /*index=5*/bf...) while((s32[]{:T(128)}, f32[128,2048]{1,0:T(8,128)S(1)}, ...), condition=%wide.region_37.38_spmd.clone, body=%wide.region_36.37_spmd.clone.sunk | while | flops 17043556 | bytes 11044691 | solution.py:33
  31.3 0.7 dynamic_slice.941
  35.9 5.6 %fusion.128 = f32[128,2048]{1,0:T(8,128)S(1)} fusion(f32[128,2048]{1,0:T(8,128)S(1)} %get-tuple-element.835, f32[2048]{0:T(1024)S(1)} %mul.1435, bf16[256,2048]{1,0:T(8,128)(2,1)S(1)} %get-tuple-element.893, s32[]{:T(128)S(6)} %select_n.1196, f32[2048]{0:T(1024)S(1)} %mul.1436, s32[]{:T(128)S(6)} %select_n.1197, f32[2048]{0:T(1024)S(1)} %mul.1437, ...), kind=kLoop, calls=%fused_computation.176.clone.1 | loop fusion | flops 17039360 | bytes 10618945 | tf_op jit(solution)/shard_map/while/body/eval_jaxpr/add | solution.py:29
  41.5 0.7 dynamic_slice.941
  46.0 5.6 %fusion.128 = f32[128,2048]{1,0:T(8,128)S(1)} fusion(f32[128,2048]{1,0:T(8,128)S(1)} %get-tuple-element.835, f32[2048]{0:T(1024)S(1)} %mul.1435, bf16[256,2048]{1,0:T(8,128)(2,1)S(1)} %get-tuple-element.893, s32[]{:T(128)S(6)} %select_n.1196, f32[2048]{0:T(1024)S(1)} %mul.1436, s32[]{:T(128)S(6)} %select_n.1197, f32[2048]{0:T(1024)S(1)} %mul.1437, ...), kind=kLoop, calls=%fused_computation.176.clone.1 | loop fusion | flops 17039360 | bytes 10618945 | tf_op jit(solution)/shard_map/while/body/eval_jaxpr/add | solution.py:29
  51.7 0.7 dynamic_slice.941
  56.2 5.6 %fusion.128 = f32[128,2048]{1,0:T(8,128)S(1)} fusion(f32[128,2048]{1,0:T(8,128)S(1)} %get-tuple-element.835, f32[2048]{0:T(1024)S(1)} %mul.1435, bf16[256,2048]{1,0:T(8,128)(2,1)S(1)} %get-tuple-element.893, s32[]{:T(128)S(6)} %select_n.1196, f32[2048]{0:T(1024)S(1)} %mul.1436, s32[]{:T(128)S(6)} %select_n.1197, f32[2048]{0:T(1024)S(1)} %mul.1437, ...), kind=kLoop, calls=%fused_computation.176.clone.1 | loop fusion | flops 17039360 | bytes 10618945 | tf_op jit(solution)/shard_map/while/body/eval_jaxpr/add | solution.py:29
  61.8 0.7 dynamic_slice.941
  66.4 5.6 %fusion.128 = f32[128,2048]{1,0:T(8,128)S(1)} fusion(f32[128,2048]{1,0:T(8,128)S(1)} %get-tuple-element.835, f32[2048]{0:T(1024)S(1)} %mul.1435, bf16[256,2048]{1,0:T(8,128)(2,1)S(1)} %get-tuple-element.893, s32[]{:T(128)S(6)} %select_n.1196, f32[2048]{0:T(1024)S(1)} %mul.1436, s32[]{:T(128)S(6)} %select_n.1197, f32[2048]{0:T(1024)S(1)} %mul.1437, ...), kind=kLoop, calls=%fused_computation.176.clone.1 | loop fusion | flops 17039360 | bytes 10618945 | tf_op jit(solution)/shard_map/while/body/eval_jaxpr/add | solution.py:29
  72.0 0.7 dynamic_slice.941
  76.5 5.6 %fusion.128 = f32[128,2048]{1,0:T(8,128)S(1)} fusion(f32[128,2048]{1,0:T(8,128)S(1)} %get-tuple-element.835, f32[2048]{0:T(1024)S(1)} %mul.1435, bf16[256,2048]{1,0:T(8,128)(2,1)S(1)} %get-tuple-element.893, s32[]{:T(128)S(6)} %select_n.1196, f32[2048]{0:T(1024)S(1)} %mul.1436, s32[]{:T(128)S(6)} %select_n.1197, f32[2048]{0:T(1024)S(1)} %mul.1437, ...), kind=kLoop, calls=%fused_computation.176.clone.1 | loop fusion | flops 17039360 | bytes 10618945 | tf_op jit(solution)/shard_map/while/body/eval_jaxpr/add | solution.py:29
  86.7 5.6 %fusion.128 = f32[128,2048]{1,0:T(8,128)S(1)} fusion(f32[128,2048]{1,0:T(8,128)S(1)} %get-tuple-element.835, f32[2048]{0:T(1024)S(1)} %mul.1435, bf16[256,2048]{1,0:T(8,128)(2,1)S(1)} %get-tuple-element.893, s32[]{:T(128)S(6)} %select_n.1196, f32[2048]{0:T(1024)S(1)} %mul.1436, s32[]{:T(128)S(6)} %select_n.1197, f32[2048]{0:T(1024)S(1)} %mul.1437, ...), kind=kLoop, calls=%fused_computation.176.clone.1 | loop fusion | flops 17039360 | bytes 10618945 | tf_op jit(solution)/shard_map/while/body/eval_jaxpr/add | solution.py:29
  96.9 5.6 %fusion.128 = f32[128,2048]{1,0:T(8,128)S(1)} fusion(f32[128,2048]{1,0:T(8,128)S(1)} %get-tuple-element.835, f32[2048]{0:T(1024)S(1)} %mul.1435, bf16[256,2048]{1,0:T(8,128)(2,1)S(1)} %get-tuple-element.893, s32[]{:T(128)S(6)} %select_n.1196, f32[2048]{0:T(1024)S(1)} %mul.1436, s32[]{:T(128)S(6)} %select_n.1197, f32[2048]{0:T(1024)S(1)} %mul.1437, ...), kind=kLoop, calls=%fused_computation.176.clone.1 | loop fusion | flops 17039360 | bytes 10618945 | tf_op jit(solution)/shard_map/while/body/eval_jaxpr/add | solution.py:29
  107.0 5.6 %fusion.128 = f32[128,2048]{1,0:T(8,128)S(1)} fusion(f32[128,2048]{1,0:T(8,128)S(1)} %get-tuple-element.835, f32[2048]{0:T(1024)S(1)} %mul.1435, bf16[256,2048]{1,0:T(8,128)(2,1)S(1)} %get-tuple-element.893, s32[]{:T(128)S(6)} %select_n.1196, f32[2048]{0:T(1024)S(1)} %mul.1436, s32[]{:T(128)S(6)} %select_n.1197, f32[2048]{0:T(1024)S(1)} %mul.1437, ...), kind=kLoop, calls=%fused_computation.176.clone.1 | loop fusion | flops 17039360 | bytes 10618945 | tf_op jit(solution)/shard_map/while/body/eval_jaxpr/add | solution.py:29
  112.7 2.6 fusion.118
  115.3 3.8 %collective-permute-start.1 = (bf16[128,2048]{1,0:T(8,128)(2,1)S(1)}, bf16[128,2048]{1,0:T(8,128)(2,1)}, u32[]{:S(2)}, u32[]{:S(2)}) collective-permute-start(bf16[128,2048]{1,0:T(8,128)(2,1)S(1)} %get-tuple-element.492), channel_id=1, source_target_pairs={{0,1},{1,2},{2,3},{3,4},{4,5},{5,6},{6,7},{7,8},{8,9},{9,10},{10,1... | collective-permute-start | bytes 1572872 | tf_op jit(solution)/shard_map/ppermute | solution.py:16
  119.4 7.5 %collective-permute-done.1 = bf16[128,2048]{1,0:T(8,128)(2,1)} collective-permute-done((bf16[128,2048]{1,0:T(8,128)(2,1)S(1)}, bf16[128,2048]{1,0:T(8,128)(2,1)}, u32[]{:S(2)}, u32[]{:S(2)}) %collective-permute-start.1) | collective-permute-done | bytes 524320 | tf_op jit(solution)/shard_map/ppermute | solution.py:16
  126.9 2.2 pad_maximum_fusion.2
  129.1 1.5 copy.17
  130.6 177.8 %while.29 = (s32[]{:T(128)}, f32[128,2048]{0,1:T(8,128)S(1)}, f32[8,16,128]{2,1,0:T(8,128)}, s32[8]{0:T(128)S(1)}, s32[128]{0:T(128)S(1)}, /*index=5*/bf16[256,2...) while((s32[]{:T(128)}, f32[128,2048]{0,1:T(8,128)S(1)}, ...), condition=%wide.region_35.36_spmd.clone, body=%wide.region_2.35_spmd.clone.sunk | while | flops 30148740 | bytes 21566524 | solution.py:79
  132.0 6.9 %bitcast_reduce_fusion.17 = (bf16[128,128]{0,1:T(8,128)(2,1)S(1)}, bf16[128,128]{0,1:T(8,128)(2,1)S(1)}, bf16[128,128]{0,1:T(8,128)(2,1)S(1)}, bf16[128,128]{0,1...) fusion(f32[128,2048]{0,1:T(8,128)S(1)} %get-tuple-element.1035,, ...), kind=kLoop, calls=%fused_computation.64.clone.1 | loop fusion | flops 12320768 | bytes 9961536 | tf_op jit(solution)/shard_map/while/body/eval_jaxpr/reduce_sum | solution.py:71
  143.3 9.6 %fusion.126 = f32[128,2048]{0,1:T(8,128)S(1)} fusion(f32[128,2048]{0,1:T(8,128)S(1)} %get-tuple-element.987, f32[2048]{0:T(1024)S(1)} %mul.1386, f32[2048]{0:T(1024)S(1)} %mul.1387, f32[2048]{0:T(1024)S(1)} %mul.1388, f32[2048]{0:T(1024)S(1)} %mul.1389, f32[2048]{0:T(1024)S(1)} %mul.1390, f32[2048]{0:T(1024)S(1)} %mul.1391, f32[2048]{0:T(1024)S(1)} %mul.1392, ...), kind=kLoop, calls=%fused_computation.48.clone.1 | loop fusion | flops 17039360 | bytes 10618945 | tf_op jit(solution)/shard_map/while/body/eval_jaxpr/add | solution.py:70
  154.2 6.9 %bitcast_reduce_fusion.17 = (bf16[128,128]{0,1:T(8,128)(2,1)S(1)}, bf16[128,128]{0,1:T(8,128)(2,1)S(1)}, bf16[128,128]{0,1:T(8,128)(2,1)S(1)}, bf16[128,128]{0,1...) fusion(f32[128,2048]{0,1:T(8,128)S(1)} %get-tuple-element.1035,, ...), kind=kLoop, calls=%fused_computation.64.clone.1 | loop fusion | flops 12320768 | bytes 9961536 | tf_op jit(solution)/shard_map/while/body/eval_jaxpr/reduce_sum | solution.py:71
  165.5 9.6 %fusion.126 = f32[128,2048]{0,1:T(8,128)S(1)} fusion(f32[128,2048]{0,1:T(8,128)S(1)} %get-tuple-element.987, f32[2048]{0:T(1024)S(1)} %mul.1386, f32[2048]{0:T(1024)S(1)} %mul.1387, f32[2048]{0:T(1024)S(1)} %mul.1388, f32[2048]{0:T(1024)S(1)} %mul.1389, f32[2048]{0:T(1024)S(1)} %mul.1390, f32[2048]{0:T(1024)S(1)} %mul.1391, f32[2048]{0:T(1024)S(1)} %mul.1392, ...), kind=kLoop, calls=%fused_computation.48.clone.1 | loop fusion | flops 17039360 | bytes 10618945 | tf_op jit(solution)/shard_map/while/body/eval_jaxpr/add | solution.py:70
  176.5 6.9 %bitcast_reduce_fusion.17 = (bf16[128,128]{0,1:T(8,128)(2,1)S(1)}, bf16[128,128]{0,1:T(8,128)(2,1)S(1)}, bf16[128,128]{0,1:T(8,128)(2,1)S(1)}, bf16[128,128]{0,1...) fusion(f32[128,2048]{0,1:T(8,128)S(1)} %get-tuple-element.1035,, ...), kind=kLoop, calls=%fused_computation.64.clone.1 | loop fusion | flops 12320768 | bytes 9961536 | tf_op jit(solution)/shard_map/while/body/eval_jaxpr/reduce_sum | solution.py:71
  187.7 9.6 %fusion.126 = f32[128,2048]{0,1:T(8,128)S(1)} fusion(f32[128,2048]{0,1:T(8,128)S(1)} %get-tuple-element.987, f32[2048]{0:T(1024)S(1)} %mul.1386, f32[2048]{0:T(1024)S(1)} %mul.1387, f32[2048]{0:T(1024)S(1)} %mul.1388, f32[2048]{0:T(1024)S(1)} %mul.1389, f32[2048]{0:T(1024)S(1)} %mul.1390, f32[2048]{0:T(1024)S(1)} %mul.1391, f32[2048]{0:T(1024)S(1)} %mul.1392, ...), kind=kLoop, calls=%fused_computation.48.clone.1 | loop fusion | flops 17039360 | bytes 10618945 | tf_op jit(solution)/shard_map/while/body/eval_jaxpr/add | solution.py:70
  198.7 6.9 %bitcast_reduce_fusion.17 = (bf16[128,128]{0,1:T(8,128)(2,1)S(1)}, bf16[128,128]{0,1:T(8,128)(2,1)S(1)}, bf16[128,128]{0,1:T(8,128)(2,1)S(1)}, bf16[128,128]{0,1...) fusion(f32[128,2048]{0,1:T(8,128)S(1)} %get-tuple-element.1035,, ...), kind=kLoop, calls=%fused_computation.64.clone.1 | loop fusion | flops 12320768 | bytes 9961536 | tf_op jit(solution)/shard_map/while/body/eval_jaxpr/reduce_sum | solution.py:71
  210.0 9.6 %fusion.126 = f32[128,2048]{0,1:T(8,128)S(1)} fusion(f32[128,2048]{0,1:T(8,128)S(1)} %get-tuple-element.987, f32[2048]{0:T(1024)S(1)} %mul.1386, f32[2048]{0:T(1024)S(1)} %mul.1387, f32[2048]{0:T(1024)S(1)} %mul.1388, f32[2048]{0:T(1024)S(1)} %mul.1389, f32[2048]{0:T(1024)S(1)} %mul.1390, f32[2048]{0:T(1024)S(1)} %mul.1391, f32[2048]{0:T(1024)S(1)} %mul.1392, ...), kind=kLoop, calls=%fused_computation.48.clone.1 | loop fusion | flops 17039360 | bytes 10618945 | tf_op jit(solution)/shard_map/while/body/eval_jaxpr/add | solution.py:70
  220.9 6.9 %bitcast_reduce_fusion.17 = (bf16[128,128]{0,1:T(8,128)(2,1)S(1)}, bf16[128,128]{0,1:T(8,128)(2,1)S(1)}, bf16[128,128]{0,1:T(8,128)(2,1)S(1)}, bf16[128,128]{0,1...) fusion(f32[128,2048]{0,1:T(8,128)S(1)} %get-tuple-element.1035,, ...), kind=kLoop, calls=%fused_computation.64.clone.1 | loop fusion | flops 12320768 | bytes 9961536 | tf_op jit(solution)/shard_map/while/body/eval_jaxpr/reduce_sum | solution.py:71
  232.2 9.6 %fusion.126 = f32[128,2048]{0,1:T(8,128)S(1)} fusion(f32[128,2048]{0,1:T(8,128)S(1)} %get-tuple-element.987, f32[2048]{0:T(1024)S(1)} %mul.1386, f32[2048]{0:T(1024)S(1)} %mul.1387, f32[2048]{0:T(1024)S(1)} %mul.1388, f32[2048]{0:T(1024)S(1)} %mul.1389, f32[2048]{0:T(1024)S(1)} %mul.1390, f32[2048]{0:T(1024)S(1)} %mul.1391, f32[2048]{0:T(1024)S(1)} %mul.1392, ...), kind=kLoop, calls=%fused_computation.48.clone.1 | loop fusion | flops 17039360 | bytes 10618945 | tf_op jit(solution)/shard_map/while/body/eval_jaxpr/add | solution.py:70
  243.1 6.9 %bitcast_reduce_fusion.17 = (bf16[128,128]{0,1:T(8,128)(2,1)S(1)}, bf16[128,128]{0,1:T(8,128)(2,1)S(1)}, bf16[128,128]{0,1:T(8,128)(2,1)S(1)}, bf16[128,128]{0,1...) fusion(f32[128,2048]{0,1:T(8,128)S(1)} %get-tuple-element.1035,, ...), kind=kLoop, calls=%fused_computation.64.clone.1 | loop fusion | flops 12320768 | bytes 9961536 | tf_op jit(solution)/shard_map/while/body/eval_jaxpr/reduce_sum | solution.py:71
  254.4 9.6 %fusion.126 = f32[128,2048]{0,1:T(8,128)S(1)} fusion(f32[128,2048]{0,1:T(8,128)S(1)} %get-tuple-element.987, f32[2048]{0:T(1024)S(1)} %mul.1386, f32[2048]{0:T(1024)S(1)} %mul.1387, f32[2048]{0:T(1024)S(1)} %mul.1388, f32[2048]{0:T(1024)S(1)} %mul.1389, f32[2048]{0:T(1024)S(1)} %mul.1390, f32[2048]{0:T(1024)S(1)} %mul.1391, f32[2048]{0:T(1024)S(1)} %mul.1392, ...), kind=kLoop, calls=%fused_computation.48.clone.1 | loop fusion | flops 17039360 | bytes 10618945 | tf_op jit(solution)/shard_map/while/body/eval_jaxpr/add | solution.py:70
  265.4 6.9 %bitcast_reduce_fusion.17 = (bf16[128,128]{0,1:T(8,128)(2,1)S(1)}, bf16[128,128]{0,1:T(8,128)(2,1)S(1)}, bf16[128,128]{0,1:T(8,128)(2,1)S(1)}, bf16[128,128]{0,1...) fusion(f32[128,2048]{0,1:T(8,128)S(1)} %get-tuple-element.1035,, ...), kind=kLoop, calls=%fused_computation.64.clone.1 | loop fusion | flops 12320768 | bytes 9961536 | tf_op jit(solution)/shard_map/while/body/eval_jaxpr/reduce_sum | solution.py:71
  276.6 9.6 %fusion.126 = f32[128,2048]{0,1:T(8,128)S(1)} fusion(f32[128,2048]{0,1:T(8,128)S(1)} %get-tuple-element.987, f32[2048]{0:T(1024)S(1)} %mul.1386, f32[2048]{0:T(1024)S(1)} %mul.1387, f32[2048]{0:T(1024)S(1)} %mul.1388, f32[2048]{0:T(1024)S(1)} %mul.1389, f32[2048]{0:T(1024)S(1)} %mul.1390, f32[2048]{0:T(1024)S(1)} %mul.1391, f32[2048]{0:T(1024)S(1)} %mul.1392, ...), kind=kLoop, calls=%fused_computation.48.clone.1 | loop fusion | flops 17039360 | bytes 10618945 | tf_op jit(solution)/shard_map/while/body/eval_jaxpr/add | solution.py:70
  287.6 6.9 %bitcast_reduce_fusion.17 = (bf16[128,128]{0,1:T(8,128)(2,1)S(1)}, bf16[128,128]{0,1:T(8,128)(2,1)S(1)}, bf16[128,128]{0,1:T(8,128)(2,1)S(1)}, bf16[128,128]{0,1...) fusion(f32[128,2048]{0,1:T(8,128)S(1)} %get-tuple-element.1035,, ...), kind=kLoop, calls=%fused_computation.64.clone.1 | loop fusion | flops 12320768 | bytes 9961536 | tf_op jit(solution)/shard_map/while/body/eval_jaxpr/reduce_sum | solution.py:71
  298.9 9.6 %fusion.126 = f32[128,2048]{0,1:T(8,128)S(1)} fusion(f32[128,2048]{0,1:T(8,128)S(1)} %get-tuple-element.987, f32[2048]{0:T(1024)S(1)} %mul.1386, f32[2048]{0:T(1024)S(1)} %mul.1387, f32[2048]{0:T(1024)S(1)} %mul.1388, f32[2048]{0:T(1024)S(1)} %mul.1389, f32[2048]{0:T(1024)S(1)} %mul.1390, f32[2048]{0:T(1024)S(1)} %mul.1391, f32[2048]{0:T(1024)S(1)} %mul.1392, ...), kind=kLoop, calls=%fused_computation.48.clone.1 | loop fusion | flops 17039360 | bytes 10618945 | tf_op jit(solution)/shard_map/while/body/eval_jaxpr/add | solution.py:70
  308.9 1.2 fusion.119
  310.3 1.9 collective-permute-start.3
  312.3 1.4 collective-permute-done.3
  313.8 2.6 fusion.111
  316.4 29.3 %all-gather.2.cloned.1.call-done = f32[16,128,128]{2,1,0:T(8,128)} async-done(((f32[1,128,128]{2,1,0:T(8,128)}), f32[16,128,128]{2,1,0:T(8,128)}) %all-gather.2.cloned.1.call-update) | async-done | bytes 1048592 | tf_op jit(solution)/shard_map/all_gather | solution.py:103
  345.7 1.3 reduce_sum.425
  (682 shorter events, 68.1 us)
Async XLA Ops:
  7.2 338.6 %all-gather.2.cloned.1.call-start = ((), (), s32[]{:S(2)}) async-start(), calls=%async_computation | async-start | bytes 1114112 | tf_op jit(solution)/shard_map/all_gather | solution.py:103
  7.2 24.1 %copy-start.5 = (bf16[1,128,128]{2,1,0:T(8,128)(2,1)S(1)}, bf16[1,128,128]{2,1,0:T(8,128)(2,1)}, u32[]{:S(2)}) copy-start(bf16[1,128,128]{2,1,0:T(8,128)(2,1)} %param.11) | copy-start | bytes 98308
  7.2 13.9 %collective-permute-start = (bf16[128,2048]{1,0:T(8,128)(2,1)}, bf16[128,2048]{1,0:T(8,128)(2,1)S(1)}, u32[]{:S(2)}, u32[]{:S(2)}) collective-permute-start(bf16[128,2048]{1,0:T(8,128)(2,1)} %bitcast.309), channel_id=1, source_target_pairs={{0,16},{16,0},{1,17},{17,1},{2,18},{18,2},{3,19},{19,3},{4,20},{20... | collective-permute-start | bytes 1572872 | tf_op jit(solution)/shard_map/ppermute | solution.py:10
  21.2 3.4 copy-start.4
  22.6 8.7 %copy-start.2 = (bf16[128,2048]{1,0:T(8,128)(2,1)}, bf16[128,2048]{1,0:T(8,128)(2,1)S(1)}, u32[]{:S(2)}) copy-start(bf16[128,2048]{1,0:T(8,128)(2,1)S(1)} %fusion.112) | copy-start | bytes 1572868
  22.6 8.6 %collective-permute-start.2 = (bf16[128,2048]{1,0:T(8,128)(2,1)S(1)}, bf16[128,2048]{1,0:T(8,128)(2,1)S(1)}, u32[]{:S(2)}, u32[]{:S(2)}) collective-permute-start(bf16[128,2048]{1,0:T(8,128)(2,1)S(1)} %fusion.112), channel_id=1, source_target_pairs={{1,0},{2,1},{3,2},{4,3},{5,4},{6,5},{7,6},{8,7},{9,8},{10,9},{11,1... | collective-permute-start | bytes 1572872 | tf_op jit(solution)/shard_map/ppermute | solution.py:16
  112.7 6.5 %copy-start.6 = (bf16[1,3,3,2048]{3,2,1,0:T(4,128)(2,1)S(1)}, bf16[1,3,3,2048]{3,2,1,0:T(4,128)(2,1)}, u32[]{:S(2)}) copy-start(bf16[1,3,3,2048]{3,2,1,0:T(4,128)(2,1)} %param.12) | copy-start | bytes 110596
  112.7 6.6 %copy-start.3 = (bf16[128,2048]{1,0:T(8,128)(2,1)S(1)}, bf16[128,2048]{1,0:T(8,128)(2,1)}, u32[]{:S(2)}) copy-start(bf16[128,2048]{1,0:T(8,128)(2,1)} %copy-done.2) | copy-start | bytes 1572868
  115.3 11.7 %collective-permute-start.1 = (bf16[128,2048]{1,0:T(8,128)(2,1)S(1)}, bf16[128,2048]{1,0:T(8,128)(2,1)}, u32[]{:S(2)}, u32[]{:S(2)}) collective-permute-start(bf16[128,2048]{1,0:T(8,128)(2,1)S(1)} %get-tuple-element.492), channel_id=1, source_target_pairs={{0,1},{1,2},{2,3},{3,4},{4,5},{5,6},{6,7},{7,8},{8,9},{9,10},{10,1... | collective-permute-start | bytes 1572872 | tf_op jit(solution)/shard_map/ppermute | solution.py:16
  308.5 1.5 copy-start
  308.5 1.5 copy-start.1
  310.3 3.4 collective-permute-start.3
Sparse Core Ops, SparseCore 0:
  308.6 37.1 all-gather.1
